TPU v7x, 32 devices: a whole 2x2x4 slice. The times are simulated.
32 devices in a mesh: dp: 8 (over z, y), mp: 4 (over x, core).
Axes of the slice: x: 2, y: 2, z: 4, core: 2. Of those that a mesh axis runs over, the one named last changes fastest.
Arguments:
- patches: bfloat16 [16384, 1024], P('dp'), may hold values from -110 to 110
- dest_owner: int32 [1024], P('dp'), may hold values from 0 to 7, as said below
- dest_slot: int32 [1024], P('dp'), may hold values from 0 to 127
- packed_image: int32 [1024], P('dp'), may hold values from -1 to 15, as said below
- w_query: bfloat16 [1024, 1024], P(None, 'mp'), may hold values from -0.328125 to 0.328125
- w_key: bfloat16 [1024, 1024], P(None, 'mp'), may hold values from -1.9375 to 1.9375
- w_value: bfloat16 [1024, 1024], P(None, 'mp'), may hold values from -0.1875 to 0.1875
- w_out: bfloat16 [1024, 1024], P('mp'), may hold values from -0.1875 to 0.1875
Outputs:
- packed_out: bfloat16 [16384, 1024], P('dp', 'mp')
- pooled_out: bfloat16 [128, 1024], P('dp', 'mp')
Inputs may be any that keep to these rules, and one draw needn't show every extreme that they name: dest_owner and dest_slot take the tiles of all indices of dp one to one onto the 128 tile slots of every packed sequence; each index of dp holds exactly 16 tiles for each packed sequence. `packed_image`: in every packed sequence the images 0, 1, 2 and so on lie on consecutive tile slots from slot 0 in the order of their numbers, each on 8 to 16 slots; fewer than 16 slots stay empty after the last image and hold -1.
All inputs are finite; a program needn't handle non-finite values.
Results may differ from a plain program's by a relative error of at most 0.0075.
Values may be sent and summed in bfloat16 or wider, within the bound.
A program may use at most 128 MiB of HBM per device.

v0:
```python
import jax
import jax.numpy as jnp
from jax import lax
from jax.sharding import PartitionSpec as P

HEAD_DIM = 64
IMG_OWN = 16
EPSILON = 1e-06


def normalize(rows):
    values = rows.astype(jnp.float32)
    centred = values - jnp.mean(values, axis=-1, keepdims=True)
    spread = jnp.mean(centred * centred, axis=-1, keepdims=True)
    return (centred * lax.rsqrt(spread + EPSILON)).astype(jnp.bfloat16)


def attend(queries, key_rows, values, allowed, present):
    scores = jnp.einsum(
        "qhd,khd->hqk", queries, key_rows, preferred_element_type=jnp.float32
    ) * HEAD_DIM ** (-0.5)
    masked = jnp.where(allowed[None], scores, -1e30)
    peak = jnp.max(masked, axis=-1, keepdims=True)
    raised = jnp.where(allowed[None], jnp.exp(scores - peak), 0.0)
    denominator = jnp.sum(raised, axis=-1, keepdims=True)
    denominator = jnp.where(present[None, :, None], denominator, 1.0)
    weights = (raised / denominator).astype(jnp.bfloat16)
    return jnp.einsum("hqk,khd->qhd", weights, values, preferred_element_type=jnp.float32).astype(
        jnp.bfloat16
    )


def whole_rows(queries, key_rows, values, segment, present):
    count_rows = queries.shape[0]
    block_rows = min(512, count_rows)

    def one_block(step_index):
        first_row = step_index * block_rows
        query_part = lax.dynamic_slice_in_dim(queries, first_row, block_rows, 0)
        segment_part = lax.dynamic_slice_in_dim(segment, first_row, block_rows, 0)
        live_rows = lax.dynamic_slice_in_dim(present, first_row, block_rows, 0)
        allowed = (segment_part[:, None] == segment[None, :]) & live_rows[:, None]
        return attend(query_part, key_rows, values, allowed, live_rows)

    outcome = lax.map(one_block, jnp.arange(count_rows // block_rows, dtype=jnp.int32))
    return outcome.reshape(count_rows, -1)


def on_device(patches, dest_owner, dest_slot, packed_image, w_query, w_key, w_value, w_out):
    senders = lax.axis_size("dp")
    splits = lax.axis_size("mp")
    slot_count = dest_owner.shape[0]
    per_owner = slot_count // senders
    tile_size = patches.shape[0] // slot_count
    full_width = patches.shape[1]
    part_width = full_width // splits
    numbers = jnp.arange(slot_count, dtype=jnp.int32)
    same_owner = dest_owner[:, None] == dest_owner[None, :]
    ranking = jnp.sum(
        (same_owner & (numbers[None, :] < numbers[:, None])).astype(jnp.int32), axis=1
    )
    position = dest_owner * per_owner + ranking
    picked = position[None, :] == numbers[:, None]
    ordering = jnp.sum(jnp.where(picked, numbers[None, :], 0), axis=1)
    slot_sent = jnp.sum(jnp.where(picked, dest_slot[None, :], 0), axis=1)
    got_slot = lax.all_to_all(slot_sent, "dp", split_axis=0, concat_axis=0, tiled=True)
    arrive = jnp.sum(jnp.where(got_slot[None, :] == numbers[:, None], numbers[None, :], 0), axis=1)
    tile_data = patches.reshape(slot_count, tile_size, full_width)
    column_start = lax.axis_index("mp") * part_width
    own_part = lax.dynamic_slice_in_dim(tile_data, column_start, part_width, 2)
    outgoing = jnp.take(own_part, ordering, axis=0).reshape(slot_count * tile_size, part_width)
    incoming = lax.all_to_all(outgoing, "dp", split_axis=0, concat_axis=0, tiled=True)
    own_cols = jnp.take(
        incoming.reshape(slot_count, tile_size, part_width), arrive, axis=0
    ).reshape(slot_count * tile_size, part_width)
    full_rows = lax.all_gather(own_cols, "mp", axis=1, tiled=True)
    count_rows = slot_count * tile_size
    segment = jnp.repeat(packed_image, tile_size)
    present = segment >= 0
    normed = normalize(full_rows)
    head_count = w_query.shape[1] // HEAD_DIM
    queries = (
        jnp.dot(normed, w_query, preferred_element_type=jnp.float32)
        .astype(jnp.bfloat16)
        .reshape(count_rows, head_count, HEAD_DIM)
    )
    key_rows = (
        jnp.dot(normed, w_key, preferred_element_type=jnp.float32)
        .astype(jnp.bfloat16)
        .reshape(count_rows, head_count, HEAD_DIM)
    )
    values = (
        jnp.dot(normed, w_value, preferred_element_type=jnp.float32)
        .astype(jnp.bfloat16)
        .reshape(count_rows, head_count, HEAD_DIM)
    )
    attended = whole_rows(queries, key_rows, values, segment, present)
    head_term = jnp.dot(attended, w_out, preferred_element_type=jnp.float32)
    summed = lax.psum_scatter(
        head_term.astype(jnp.bfloat16), "mp", scatter_dimension=1, tiled=True
    ).astype(jnp.float32)
    result_rows = jnp.where(present[:, None], own_cols.astype(jnp.float32) + summed, 0.0)
    packed_out = result_rows.astype(jnp.bfloat16)
    labels = jnp.arange(IMG_OWN, dtype=jnp.int32)
    member = (segment[None, :] == labels[:, None]).astype(jnp.float32)
    sums = jnp.dot(member, result_rows, precision=lax.Precision.HIGHEST)
    image_rows = jnp.sum(member, axis=1)
    filled = image_rows > 0
    pooled = sums / jnp.maximum(image_rows, 1.0)[:, None]
    local_sum = jnp.sum(jnp.where(filled[:, None], pooled, 0.0), axis=0)
    local_count = jnp.sum(filled.astype(jnp.float32))
    grand_total, number = lax.psum((local_sum, local_count), "dp")
    centre = grand_total / number
    pooled_out = jnp.where(filled[:, None], pooled - centre[None, :], 0.0).astype(jnp.bfloat16)
    return (packed_out, pooled_out)


def solution(mesh):
    in_specs = (
        P("dp", None),
        P("dp"),
        P("dp"),
        P("dp"),
        P(None, "mp"),
        P(None, "mp"),
        P(None, "mp"),
        P("mp", None),
    )
    out_specs = (P("dp", "mp"), P("dp", "mp"))
    return jax.shard_map(
        on_device, mesh=mesh, in_specs=in_specs, out_specs=out_specs, check_vma=False
    )
```

profile of v0, /device:TPU:0, one launch (start us, length us, event | category | flops | bytes accessed | tf_op | source)
XLA Modules:
  0.0 283.8 jit_solution(2327120010386773633)
XLA Ops:
  7.2 0.9 convert_reduce_fusion.2
  10.2 7.3 %all-to-all-start.1 = ((s32[8,16,1]{1,2,0:T(1,128)}), s32[8,16,1]{1,2,0:T(1,128)S(1)}, u32[]{:S(2)}, u32[]{:S(2)}) async-start(s32[8,16,1]{1,2,0:T(1,128)} %bitcast), calls=%async_computation.1 | async-start | bytes 8192 | tf_op jit(solution)/shard_map/all_to_all | solution.py:66
  17.5 1.3 constant_dynamic-slice_fusion
  19.5 1.2 broadcast_select_fusion.2
  20.7 3.2 %all-to-all-done.1 = s32[8,16,1]{1,2,0:T(1,128)S(1)} async-done(((s32[8,16,1]{1,2,0:T(1,128)}), s32[8,16,1]{1,2,0:T(1,128)S(1)}, u32[]{:S(2)}, u32[]{:S(2)}) %all-to-all-start.1) | async-done | bytes 544 | tf_op jit(solution)/shard_map/all_to_all | solution.py:66
  23.9 3.6 %all-to-all-start = ((bf16[8,256,256]{2,1,0:T(8,128)(2,1)}), bf16[8,256,256]{2,1,0:T(8,128)(2,1)S(1)}, u32[]{:S(2)}, u32[]{:S(2)}) async-start(bf16[8,256,256]{2,1,0:T(8,128)(2,1)} %bitcast.2), calls=%async_computation | async-start | bytes 2097152 | tf_op jit(solution)/shard_map/all_to_all | solution.py:72
  29.0 23.3 %all-to-all-done = bf16[8,256,256]{2,1,0:T(8,128)(2,1)S(1)} async-done(((bf16[8,256,256]{2,1,0:T(8,128)(2,1)}), bf16[8,256,256]{2,1,0:T(8,128)(2,1)S(1)}, u32[]{:S(2)}, u32[]{:S(2)}) %all-to-all-start) | async-done | bytes 1048608 | tf_op jit(solution)/shard_map/all_to_all | solution.py:72
  52.9 1.2 broadcast_select_fusion.1
  54.3 33.8 %all-gather.2.cloned.1.call-done = bf16[2048,1024]{1,0:T(8,128)(2,1)} async-done(((bf16[2048,256]{1,0:T(8,128)(2,1)}), bf16[2048,1024]{1,0:T(8,128)(2,1)}) %all-gather.2.cloned.1.call-update) | async-done | bytes 4194320 | tf_op jit(solution)/shard_map/all_gather | solution.py:76
  88.1 3.0 %convert_reduce_fusion = f32[2048]{0:T(1024)S(1)} fusion(bf16[2048,1024]{1,0:T(8,128)(2,1)} %all-gather.2.cloned.1.call-done), kind=kLoop, calls=%fused_computation.27 | loop fusion | flops 4192256 | bytes 4202496 | tf_op jit(solution)/shard_map/reduce_sum | solution.py:13
  91.5 1.4 fusion.31
  92.9 1.1 fusion.32
  94.1 2.3 convolution_convert_fusion.3
  96.4 2.3 convolution_convert_fusion.2
  98.8 2.3 convolution_convert_fusion.1
  101.1 99.0 %while.11 = (s32[]{:T(128)}, bf16[4,512,4,64]{1,3,2,0:T(8,128)(2,1)S(1)}, s32[4]{0:T(128)S(1)}, s32[2048]{0:T(1024)S(1)}, pred[2048]{0:T(1024)(128)(4,1)S(1)}, /...) while((s32[]{:T(128)}, ...), condition=%wide.region_9.11_spmd.clone, body=%wide.region_6.0_spmd.clone.sunk | while | flops 1646399488 | bytes 40707776 | solution.py:45
  102.8 0.8 compare_and_fusion.4
  103.5 13.5 %fusion.69 = (f32[4,512]{1,0:T(4,128)S(1)}, f32[4,512,2048]{2,1,0:T(8,128)}) fusion(pred[512,2048]{1,0:T(8,128)(4,1)S(1)} %compare_and_fusion.4, bf16[2048,4,64]{0,2,1:T(8,128)(2,1)} %get-tuple-element.191, bf16[2048,4,64]{0,2,1:T(8,128)(2,1)} %get-tuple-element.190, s32[]{:T(128)S(6)} %select_n.104), kind=kOutput, calls=%fused_computation.73.clone.1 | convolution fusion | flops 1098909696 | bytes 21505024 | tf_op jit(solution)/shard_map/while/body/eval_jaxpr/sub | solution.py:24
  117.0 8.7 %fusion.70 = bf16[4,512,4,64]{1,3,2,0:T(8,128)(2,1)S(1)} fusion(bf16[4,512,4,64]{1,3,2,0:T(8,128)(2,1)S(1)} %get-tuple-element.173, s32[]{:T(128)} %get-tuple-element.172, bf16[2048,4,64]{0,2,1:T(8,128)(2,1)} %get-tuple-element.192, f32[4,512,2048]{2,1,0:T(8,128)} %get-tuple-element.157, f32[4,512]{1,0:T(4,128)S(1)} %broadcast_select_fusion.4), kind=kOutput, calls=%fused_computation.17.clone.1 | convolution fusion | flops 545390592 | bytes 18096132 | tf_op jit(solution)/shard_map/while/body/eval_jaxpr/hqk,khd->qhd/dot_general | solution.py:28
  127.5 0.8 compare_and_fusion.4
  128.3 13.5 %fusion.69 = (f32[4,512]{1,0:T(4,128)S(1)}, f32[4,512,2048]{2,1,0:T(8,128)}) fusion(pred[512,2048]{1,0:T(8,128)(4,1)S(1)} %compare_and_fusion.4, bf16[2048,4,64]{0,2,1:T(8,128)(2,1)} %get-tuple-element.191, bf16[2048,4,64]{0,2,1:T(8,128)(2,1)} %get-tuple-element.190, s32[]{:T(128)S(6)} %select_n.104), kind=kOutput, calls=%fused_computation.73.clone.1 | convolution fusion | flops 1098909696 | bytes 21505024 | tf_op jit(solution)/shard_map/while/body/eval_jaxpr/sub | solution.py:24
  141.8 8.7 %fusion.70 = bf16[4,512,4,64]{1,3,2,0:T(8,128)(2,1)S(1)} fusion(bf16[4,512,4,64]{1,3,2,0:T(8,128)(2,1)S(1)} %get-tuple-element.173, s32[]{:T(128)} %get-tuple-element.172, bf16[2048,4,64]{0,2,1:T(8,128)(2,1)} %get-tuple-element.192, f32[4,512,2048]{2,1,0:T(8,128)} %get-tuple-element.157, f32[4,512]{1,0:T(4,128)S(1)} %broadcast_select_fusion.4), kind=kOutput, calls=%fused_computation.17.clone.1 | convolution fusion | flops 545390592 | bytes 18096132 | tf_op jit(solution)/shard_map/while/body/eval_jaxpr/hqk,khd->qhd/dot_general | solution.py:28
  153.0 13.6 %fusion.69 = (f32[4,512]{1,0:T(4,128)S(1)}, f32[4,512,2048]{2,1,0:T(8,128)}) fusion(pred[512,2048]{1,0:T(8,128)(4,1)S(1)} %compare_and_fusion.4, bf16[2048,4,64]{0,2,1:T(8,128)(2,1)} %get-tuple-element.191, bf16[2048,4,64]{0,2,1:T(8,128)(2,1)} %get-tuple-element.190, s32[]{:T(128)S(6)} %select_n.104), kind=kOutput, calls=%fused_computation.73.clone.1 | convolution fusion | flops 1098909696 | bytes 21505024 | tf_op jit(solution)/shard_map/while/body/eval_jaxpr/sub | solution.py:24
  166.6 8.7 %fusion.70 = bf16[4,512,4,64]{1,3,2,0:T(8,128)(2,1)S(1)} fusion(bf16[4,512,4,64]{1,3,2,0:T(8,128)(2,1)S(1)} %get-tuple-element.173, s32[]{:T(128)} %get-tuple-element.172, bf16[2048,4,64]{0,2,1:T(8,128)(2,1)} %get-tuple-element.192, f32[4,512,2048]{2,1,0:T(8,128)} %get-tuple-element.157, f32[4,512]{1,0:T(4,128)S(1)} %broadcast_select_fusion.4), kind=kOutput, calls=%fused_computation.17.clone.1 | convolution fusion | flops 545390592 | bytes 18096132 | tf_op jit(solution)/shard_map/while/body/eval_jaxpr/hqk,khd->qhd/dot_general | solution.py:28
  177.8 13.5 %fusion.69 = (f32[4,512]{1,0:T(4,128)S(1)}, f32[4,512,2048]{2,1,0:T(8,128)}) fusion(pred[512,2048]{1,0:T(8,128)(4,1)S(1)} %compare_and_fusion.4, bf16[2048,4,64]{0,2,1:T(8,128)(2,1)} %get-tuple-element.191, bf16[2048,4,64]{0,2,1:T(8,128)(2,1)} %get-tuple-element.190, s32[]{:T(128)S(6)} %select_n.104), kind=kOutput, calls=%fused_computation.73.clone.1 | convolution fusion | flops 1098909696 | bytes 21505024 | tf_op jit(solution)/shard_map/while/body/eval_jaxpr/sub | solution.py:24
  191.3 8.7 %fusion.70 = bf16[4,512,4,64]{1,3,2,0:T(8,128)(2,1)S(1)} fusion(bf16[4,512,4,64]{1,3,2,0:T(8,128)(2,1)S(1)} %get-tuple-element.173, s32[]{:T(128)} %get-tuple-element.172, bf16[2048,4,64]{0,2,1:T(8,128)(2,1)} %get-tuple-element.192, f32[4,512,2048]{2,1,0:T(8,128)} %get-tuple-element.157, f32[4,512]{1,0:T(4,128)S(1)} %broadcast_select_fusion.4), kind=kOutput, calls=%fused_computation.17.clone.1 | convolution fusion | flops 545390592 | bytes 18096132 | tf_op jit(solution)/shard_map/while/body/eval_jaxpr/hqk,khd->qhd/dot_general | solution.py:28
  200.0 0.8 copy.14
  201.1 3.2 %convolution_convert_fusion = bf16[2048,1024]{1,0:T(8,128)(2,1)} fusion(bf16[2048,256]{0,1:T(8,128)(2,1)S(1)} %bitcast.45, bf16[256,1024]{1,0:T(8,128)(2,1)S(1)} %copy-done), kind=kOutput, calls=%fused_computation.32 | convolution fusion | flops 1075838976 | bytes 5767168 | tf_op jit(solution)/shard_map/dot_general | solution.py:98
  205.1 43.8 %reduce-scatter.2.cloned.1.call-done = bf16[2048,256]{1,0:T(8,128)(2,1)} async-done(((bf16[2048,1024]{1,0:T(8,128)(2,1)}), bf16[2048,256]{1,0:T(8,128)(2,1)}) %reduce-scatter.2.cloned.1.call-update) | async-done | bytes 1048592 | tf_op jit(solution)/shard_map/reduce_scatter | solution.py:99
  248.9 2.4 select_reduce_fusion.4
  251.4 22.0 %all-reduce = (f32[256]{0:T(256)S(1)}, f32[]{:T(128)}) all-reduce(f32[256]{0:T(256)S(1)} %get-tuple-element.98, f32[]{:T(128)} %get-tuple-element.96), channel_id=1, replica_groups=mesh['dp'=8,'mp'=4] {'dp'}, use_global_device_ids=true, to_apply=%region_13.15 | all-reduce | flops 257 | bytes 2056 | tf_op jit(solution)/shard_map/psum | solution.py:112
  274.7 2.3 fusion.34
  (72 shorter events, 13.5 us)
Async XLA Ops:
  7.2 194.0 %copy-start = (bf16[256,1024]{1,0:T(8,128)(2,1)S(1)}, bf16[256,1024]{1,0:T(8,128)(2,1)}, u32[]{:S(2)}) copy-start(bf16[256,1024]{1,0:T(8,128)(2,1)} %param.19) | copy-start | bytes 1572868
  10.2 13.7 %all-to-all-start.1 = ((s32[8,16,1]{1,2,0:T(1,128)}), s32[8,16,1]{1,2,0:T(1,128)S(1)}, u32[]{:S(2)}, u32[]{:S(2)}) async-start(s32[8,16,1]{1,2,0:T(1,128)} %bitcast), calls=%async_computation.1 | async-start | bytes 8192 | tf_op jit(solution)/shard_map/all_to_all | solution.py:66
  20.7 33.5 %copy-start.3 = (s32[128]{0:T(128)S(1)}, s32[128]{0:T(128)}, u32[]{:S(2)}) copy-start(s32[128]{0:T(128)} %param.15) | copy-start | bytes 1540
  23.9 28.3 %all-to-all-start = ((bf16[8,256,256]{2,1,0:T(8,128)(2,1)}), bf16[8,256,256]{2,1,0:T(8,128)(2,1)S(1)}, u32[]{:S(2)}, u32[]{:S(2)}) async-start(bf16[8,256,256]{2,1,0:T(8,128)(2,1)} %bitcast.2), calls=%async_computation | async-start | bytes 2097152 | tf_op jit(solution)/shard_map/all_to_all | solution.py:72
  27.5 60.6 %all-gather.2.cloned.1.call-start = ((), (), s32[]{:S(2)}) async-start(), calls=%async_computation.3 | async-start | bytes 5242880 | tf_op jit(solution)/shard_map/all_gather | solution.py:76
  54.1 194.9 %reduce-scatter.2.cloned.1.call-start = ((), (), s32[]{:S(2)}) async-start(), calls=%async_computation.4 | async-start | bytes 5242880 | tf_op jit(solution)/shard_map/reduce_scatter | solution.py:99
  88.1 3.4 %copy-start.1 = (bf16[2048,1024]{1,0:T(8,128)(2,1)S(1)}, bf16[2048,1024]{1,0:T(8,128)(2,1)}, u32[]{:S(2)}) copy-start(bf16[2048,1024]{1,0:T(8,128)(2,1)} %all-gather.2.cloned.1.call-done) | copy-start | bytes 12582916
  92.9 1.2 copy-start.4
  94.1 2.3 copy-start.5
  96.4 2.4 copy-start.6
  204.4 44.6 %copy-start.2 = (bf16[128,16,256]{2,1,0:T(8,128)(2,1)S(1)}, bf16[128,16,256]{2,1,0:T(8,128)(2,1)}, u32[]{:S(2)}) copy-start(bf16[128,16,256]{2,1,0:T(8,128)(2,1)} %broadcast_select_fusion.1) | copy-start | bytes 3145732
Sparse Core Ops, SparseCore 0:
  54.2 33.8 all-gather.1
  204.5 44.3 reduce-scatter.1
where the time goes:
time: 284 us
  waiting for transfers between devices  104 us (37%)
  matrix products  102 us (36%)
  blocking collectives  22 us (8%)
  other arithmetic  18.4 us (6%)
  between operations  14.3 us (5%)
  starting transfers between devices  11 us (4%)
  local copies, waits for them, and re-layouts  9.55 us (3%)
  loops' own time  2.92 us (1%)
    sub x4, matrix products, attend(): raised = jnp.where(allowed[None], jnp.exp(scores - peak), 0.0)  54.1 us
    reduce_scatter x1, waiting for transfers between devices, on_device(): lax.psum_scatter(head_term.astype(jnp.bfloat16), 'mp', scatter_dimension=...  43.8 us
    dot_general x4, matrix products, attend(): jnp.einsum('hqk,khd->qhd', weights, values, preferred_element_type=jnp.fl...  34.9 us
    all_gather x1, waiting for transfers between devices, on_device(): full_rows = lax.all_gather(own_cols, 'mp', axis=1, tiled=True)  33.8 us
    all_to_all x1, waiting for transfers between devices, on_device(): lax.all_to_all(outgoing, 'dp', split_axis=0, concat_axis=0, tiled=True)  23.3 us
    psum x1, blocking collectives, on_device(): grand_total, number = lax.psum((local_sum, local_count), 'dp')  22 us
    all_to_all x1, starting transfers between devices, on_device(): lax.all_to_all(slot_sent, 'dp', split_axis=0, concat_axis=0, tiled=True)  7.31 us
  transfers between devices with their start and end apart: 4, of which 4 were waited for; matrix products, arithmetic and copies ran while one was open for 2% of the time, Pallas kernels for 0%

commit v1 on v0

--- a/solution.py
+++ b/solution.py
@@ -73,7 +73,12 @@
     own_cols = jnp.take(
         incoming.reshape(slot_count, tile_size, part_width), arrive, axis=0
     ).reshape(slot_count * tile_size, part_width)
-    full_rows = lax.all_gather(own_cols, "mp", axis=1, tiled=True)
+    ring = [own_cols]
+    for hop in range(3):
+        ring.append(lax.ppermute(ring[-1], "mp", [(dev, (dev + 1) % 4) for dev in range(4)]))
+    full_rows = jnp.roll(
+        jnp.concatenate(ring[::-1], axis=1), (lax.axis_index("mp") + 1) * ring[0].shape[1], axis=1
+    )
     count_rows = slot_count * tile_size
     segment = jnp.repeat(packed_image, tile_size)
     present = segment >= 0

time: 284 us -> 295 us (1.039)
  waiting for transfers between devices: 104 us -> 112 us
  local copies, waits for them, and re-layouts: 9.55 us -> 14.8 us
  other arithmetic: 18.4 us -> 15.2 us
    ppermute x0 -> x3, waiting for transfers between devices: none -> 42.9 us  [on_device(): lax.ppermute(ring[-1], 'mp', [(dev, (dev + 1) % 4) for dev in range(4)])]
    all_gather x1 -> x0, waiting for transfers between devices: 33.8 us -> none  [on_device(): full_rows = lax.all_gather(own_cols, 'mp', axis=1, tiled=True)]
    unnamed x15 -> x24, local copies, waits for them, and re-layouts: 0.78 us -> 6.19 us
  transfers between devices with their start and end apart: 4 -> 6, of which waited for: 4 -> 6; matrix products, arithmetic and copies ran while one was open for 2% -> 2% of each run, Pallas kernels for 0% -> 0%
where the time goes in v1:
time: 295 us; the launch traced here: 294 us
  waiting for transfers between devices  112 us (38%)
  matrix products  102 us (35%)
  blocking collectives  22 us (7%)
  other arithmetic  15.2 us (5%)
  local copies, waits for them, and re-layouts  14.8 us (5%)
  between operations  14.4 us (5%)
  starting transfers between devices  11 us (4%)
    sub x4, matrix products, attend(): raised = jnp.where(allowed[None], jnp.exp(scores - peak), 0.0)  54.3 us
    ppermute x3, waiting for transfers between devices, on_device(): lax.ppermute(ring[-1], 'mp', [(dev, (dev + 1) % 4) for dev in range(4)])  42.9 us
    reduce_scatter x1, waiting for transfers between devices, on_device(): lax.psum_scatter(head_term.astype(jnp.bfloat16), 'mp', scatter_dimension=...  42.6 us
    dot_general x4, matrix products, attend(): jnp.einsum('hqk,khd->qhd', weights, values, preferred_element_type=jnp.fl...  34.9 us
    all_to_all x1, waiting for transfers between devices, on_device(): lax.all_to_all(outgoing, 'dp', split_axis=0, concat_axis=0, tiled=True)  23.3 us
    psum x1, blocking collectives, on_device(): grand_total, number = lax.psum((local_sum, local_count), 'dp')  22 us
    all_to_all x1, starting transfers between devices, on_device(): lax.all_to_all(slot_sent, 'dp', split_axis=0, concat_axis=0, tiled=True)  7.31 us
    unnamed x24, local copies, waits for them, and re-layouts  6.19 us
  transfers between devices with their start and end apart: 6, of which 6 were waited for; matrix products, arithmetic and copies ran while one was open for 2% of the time, Pallas kernels for 0%

profile of v1, /device:TPU:0, one launch (start us, length us, event | category | flops | bytes accessed | tf_op | source)
XLA Modules:
  0.0 293.8 jit_solution(592984040308212447)
XLA Ops:
  10.2 7.3 %all-to-all-start.1 = ((s32[8,16,1]{1,2,0:T(1,128)}), s32[8,16,1]{1,2,0:T(1,128)S(1)}, u32[]{:S(2)}, u32[]{:S(2)}) async-start(s32[8,16,1]{1,2,0:T(1,128)} %bitcast), calls=%async_computation.1 | async-start | bytes 8192 | tf_op jit(solution)/shard_map/all_to_all | solution.py:66
  17.6 1.3 constant_dynamic-slice_fusion
  19.5 1.2 broadcast_select_fusion.2
  20.7 3.2 %all-to-all-done.1 = s32[8,16,1]{1,2,0:T(1,128)S(1)} async-done(((s32[8,16,1]{1,2,0:T(1,128)}), s32[8,16,1]{1,2,0:T(1,128)S(1)}, u32[]{:S(2)}, u32[]{:S(2)}) %all-to-all-start.1) | async-done | bytes 544 | tf_op jit(solution)/shard_map/all_to_all | solution.py:66
  23.9 3.6 %all-to-all-start = ((bf16[8,256,256]{2,1,0:T(8,128)(2,1)}), bf16[8,256,256]{2,1,0:T(8,128)(2,1)S(1)}, u32[]{:S(2)}, u32[]{:S(2)}) async-start(bf16[8,256,256]{2,1,0:T(8,128)(2,1)} %bitcast.2), calls=%async_computation | async-start | bytes 2097152 | tf_op jit(solution)/shard_map/all_to_all | solution.py:72
  29.0 23.3 %all-to-all-done = bf16[8,256,256]{2,1,0:T(8,128)(2,1)S(1)} async-done(((bf16[8,256,256]{2,1,0:T(8,128)(2,1)}), bf16[8,256,256]{2,1,0:T(8,128)(2,1)S(1)}, u32[]{:S(2)}, u32[]{:S(2)}) %all-to-all-start) | async-done | bytes 1048608 | tf_op jit(solution)/shard_map/all_to_all | solution.py:72
  53.2 14.2 %collective-permute-done = bf16[2048,256]{1,0:T(8,128)(2,1)S(1)} collective-permute-done((bf16[2048,256]{1,0:T(8,128)(2,1)S(1)}, bf16[2048,256]{1,0:T(8,128)(2,1)S(1)}, u32[]{:S(2)}, u32[]{:S(2)}) %collective-permute-start) | collective-permute-done | bytes 1048608 | tf_op jit(solution)/shard_map/ppermute | solution.py:78
  67.4 14.3 %collective-permute-done.1 = bf16[2048,256]{1,0:T(8,128)(2,1)} collective-permute-done((bf16[2048,256]{1,0:T(8,128)(2,1)S(1)}, bf16[2048,256]{1,0:T(8,128)(2,1)}, u32[]{:S(2)}, u32[]{:S(2)}) %collective-permute-start.1) | collective-permute-done | bytes 1048608 | tf_op jit(solution)/shard_map/ppermute | solution.py:78
  81.9 14.4 %collective-permute-done.2 = bf16[2048,256]{1,0:T(8,128)(2,1)} collective-permute-done((bf16[2048,256]{1,0:T(8,128)(2,1)}, bf16[2048,256]{1,0:T(8,128)(2,1)}, u32[]{:S(2)}, u32[]{:S(2)}) %collective-permute-start.2) | collective-permute-done | bytes 1048608 | tf_op jit(solution)/shard_map/ppermute | solution.py:78
  96.3 1.4 constant_dynamic-update-slice_fusion.7
  97.6 1.4 constant_dynamic-update-slice_fusion.6
  99.3 1.4 constant_dynamic-update-slice_fusion.3
  100.7 1.4 constant_dynamic-update-slice_fusion.2
  103.0 1.4 fusion.31
  104.4 1.1 fusion.32
  105.6 2.4 convolution_convert_fusion.3
  107.9 2.3 convolution_convert_fusion.2
  110.3 2.3 convolution_convert_fusion.1
  112.6 98.7 %while.11 = (s32[]{:T(128)}, bf16[4,512,4,64]{1,3,2,0:T(8,128)(2,1)S(1)}, s32[4]{0:T(128)S(1)}, s32[2048]{0:T(1024)S(1)}, pred[2048]{0:T(1024)(128)(4,1)S(1)}, /...) while((s32[]{:T(128)}, ...), condition=%wide.region_9.11_spmd.clone, body=%wide.region_6.10_spmd.clone.sunk | while | flops 1646399488 | bytes 40707776 | solution.py:45
  114.9 13.5 %fusion.69 = (f32[4,512]{1,0:T(4,128)S(1)}, f32[4,512,2048]{2,1,0:T(8,128)}) fusion(pred[512,2048]{1,0:T(8,128)(4,1)S(1)} %compare_and_fusion.4, bf16[2048,4,64]{0,2,1:T(8,128)(2,1)} %get-tuple-element.191, bf16[2048,4,64]{0,2,1:T(8,128)(2,1)} %get-tuple-element.190, s32[]{:T(128)S(6)} %select_n.119), kind=kOutput, calls=%fused_computation.81.clone.1 | convolution fusion | flops 1098909696 | bytes 21505024 | tf_op jit(solution)/shard_map/while/body/eval_jaxpr/sub | solution.py:24
  128.4 8.7 %fusion.70 = bf16[4,512,4,64]{1,3,2,0:T(8,128)(2,1)S(1)} fusion(bf16[4,512,4,64]{1,3,2,0:T(8,128)(2,1)S(1)} %get-tuple-element.173, s32[]{:T(128)} %get-tuple-element.172, bf16[2048,4,64]{0,2,1:T(8,128)(2,1)} %get-tuple-element.192, f32[4,512,2048]{2,1,0:T(8,128)} %get-tuple-element.157, f32[4,512]{1,0:T(4,128)S(1)} %broadcast_select_fusion.4), kind=kOutput, calls=%fused_computation.17.clone.1 | convolution fusion | flops 545390592 | bytes 18096132 | tf_op jit(solution)/shard_map/while/body/eval_jaxpr/hqk,khd->qhd/dot_general | solution.py:28
  139.5 13.7 %fusion.69 = (f32[4,512]{1,0:T(4,128)S(1)}, f32[4,512,2048]{2,1,0:T(8,128)}) fusion(pred[512,2048]{1,0:T(8,128)(4,1)S(1)} %compare_and_fusion.4, bf16[2048,4,64]{0,2,1:T(8,128)(2,1)} %get-tuple-element.191, bf16[2048,4,64]{0,2,1:T(8,128)(2,1)} %get-tuple-element.190, s32[]{:T(128)S(6)} %select_n.119), kind=kOutput, calls=%fused_computation.81.clone.1 | convolution fusion | flops 1098909696 | bytes 21505024 | tf_op jit(solution)/shard_map/while/body/eval_jaxpr/sub | solution.py:24
  153.2 8.7 %fusion.70 = bf16[4,512,4,64]{1,3,2,0:T(8,128)(2,1)S(1)} fusion(bf16[4,512,4,64]{1,3,2,0:T(8,128)(2,1)S(1)} %get-tuple-element.173, s32[]{:T(128)} %get-tuple-element.172, bf16[2048,4,64]{0,2,1:T(8,128)(2,1)} %get-tuple-element.192, f32[4,512,2048]{2,1,0:T(8,128)} %get-tuple-element.157, f32[4,512]{1,0:T(4,128)S(1)} %broadcast_select_fusion.4), kind=kOutput, calls=%fused_computation.17.clone.1 | convolution fusion | flops 545390592 | bytes 18096132 | tf_op jit(solution)/shard_map/while/body/eval_jaxpr/hqk,khd->qhd/dot_general | solution.py:28
  164.3 13.6 %fusion.69 = (f32[4,512]{1,0:T(4,128)S(1)}, f32[4,512,2048]{2,1,0:T(8,128)}) fusion(pred[512,2048]{1,0:T(8,128)(4,1)S(1)} %compare_and_fusion.4, bf16[2048,4,64]{0,2,1:T(8,128)(2,1)} %get-tuple-element.191, bf16[2048,4,64]{0,2,1:T(8,128)(2,1)} %get-tuple-element.190, s32[]{:T(128)S(6)} %select_n.119), kind=kOutput, calls=%fused_computation.81.clone.1 | convolution fusion | flops 1098909696 | bytes 21505024 | tf_op jit(solution)/shard_map/while/body/eval_jaxpr/sub | solution.py:24
  177.9 8.7 %fusion.70 = bf16[4,512,4,64]{1,3,2,0:T(8,128)(2,1)S(1)} fusion(bf16[4,512,4,64]{1,3,2,0:T(8,128)(2,1)S(1)} %get-tuple-element.173, s32[]{:T(128)} %get-tuple-element.172, bf16[2048,4,64]{0,2,1:T(8,128)(2,1)} %get-tuple-element.192, f32[4,512,2048]{2,1,0:T(8,128)} %get-tuple-element.157, f32[4,512]{1,0:T(4,128)S(1)} %broadcast_select_fusion.4), kind=kOutput, calls=%fused_computation.17.clone.1 | convolution fusion | flops 545390592 | bytes 18096132 | tf_op jit(solution)/shard_map/while/body/eval_jaxpr/hqk,khd->qhd/dot_general | solution.py:28
  189.0 13.5 %fusion.69 = (f32[4,512]{1,0:T(4,128)S(1)}, f32[4,512,2048]{2,1,0:T(8,128)}) fusion(pred[512,2048]{1,0:T(8,128)(4,1)S(1)} %compare_and_fusion.4, bf16[2048,4,64]{0,2,1:T(8,128)(2,1)} %get-tuple-element.191, bf16[2048,4,64]{0,2,1:T(8,128)(2,1)} %get-tuple-element.190, s32[]{:T(128)S(6)} %select_n.119), kind=kOutput, calls=%fused_computation.81.clone.1 | convolution fusion | flops 1098909696 | bytes 21505024 | tf_op jit(solution)/shard_map/while/body/eval_jaxpr/sub | solution.py:24
  202.5 8.7 %fusion.70 = bf16[4,512,4,64]{1,3,2,0:T(8,128)(2,1)S(1)} fusion(bf16[4,512,4,64]{1,3,2,0:T(8,128)(2,1)S(1)} %get-tuple-element.173, s32[]{:T(128)} %get-tuple-element.172, bf16[2048,4,64]{0,2,1:T(8,128)(2,1)} %get-tuple-element.192, f32[4,512,2048]{2,1,0:T(8,128)} %get-tuple-element.157, f32[4,512]{1,0:T(4,128)S(1)} %broadcast_select_fusion.4), kind=kOutput, calls=%fused_computation.17.clone.1 | convolution fusion | flops 545390592 | bytes 18096132 | tf_op jit(solution)/shard_map/while/body/eval_jaxpr/hqk,khd->qhd/dot_general | solution.py:28
  212.3 3.2 %convolution_convert_fusion = bf16[2048,1024]{1,0:T(8,128)(2,1)} fusion(bf16[2048,256]{0,1:T(8,128)(2,1)S(1)} %bitcast.47, bf16[256,1024]{1,0:T(8,128)(2,1)S(1)} %copy-done), kind=kOutput, calls=%fused_computation.32 | convolution fusion | flops 1075838976 | bytes 5767168 | tf_op jit(solution)/shard_map/dot_general | solution.py:103
  216.3 42.6 %reduce-scatter.2.cloned.1.call-done = bf16[2048,256]{1,0:T(8,128)(2,1)} async-done(((bf16[2048,1024]{1,0:T(8,128)(2,1)}), bf16[2048,256]{1,0:T(8,128)(2,1)}) %reduce-scatter.2.cloned.1.call-update) | async-done | bytes 1048592 | tf_op jit(solution)/shard_map/reduce_scatter | solution.py:104
  259.0 2.4 select_reduce_fusion.4
  261.4 22.0 %all-reduce = (f32[256]{0:T(256)S(1)}, f32[]{:T(128)}) all-reduce(f32[256]{0:T(256)S(1)} %get-tuple-element.98, f32[]{:T(128)} %get-tuple-element.96), channel_id=1, replica_groups=mesh['dp'=8,'mp'=4] {'dp'}, use_global_device_ids=true, to_apply=%region_13.15 | all-reduce | flops 257 | bytes 2056 | tf_op jit(solution)/shard_map/psum | solution.py:117
  284.7 2.3 fusion.34
  (85 shorter events, 17.3 us)
Async XLA Ops:
  7.2 205.2 %copy-start = (bf16[256,1024]{1,0:T(8,128)(2,1)S(1)}, bf16[256,1024]{1,0:T(8,128)(2,1)}, u32[]{:S(2)}) copy-start(bf16[256,1024]{1,0:T(8,128)(2,1)} %param.19) | copy-start | bytes 1572868
  7.2 74.5 %copy-start.4 = (s32[128]{0:T(128)S(1)}, s32[128]{0:T(128)}, u32[]{:S(2)}) copy-start(s32[128]{0:T(128)} %param.15) | copy-start | bytes 1540
  10.2 13.7 %all-to-all-start.1 = ((s32[8,16,1]{1,2,0:T(1,128)}), s32[8,16,1]{1,2,0:T(1,128)S(1)}, u32[]{:S(2)}, u32[]{:S(2)}) async-start(s32[8,16,1]{1,2,0:T(1,128)} %bitcast), calls=%async_computation.1 | async-start | bytes 8192 | tf_op jit(solution)/shard_map/all_to_all | solution.py:66
  23.9 28.3 %all-to-all-start = ((bf16[8,256,256]{2,1,0:T(8,128)(2,1)}), bf16[8,256,256]{2,1,0:T(8,128)(2,1)S(1)}, u32[]{:S(2)}, u32[]{:S(2)}) async-start(bf16[8,256,256]{2,1,0:T(8,128)(2,1)} %bitcast.2), calls=%async_computation | async-start | bytes 2097152 | tf_op jit(solution)/shard_map/all_to_all | solution.py:72
  27.5 231.5 %reduce-scatter.2.cloned.1.call-start = ((), (), s32[]{:S(2)}) async-start(), calls=%async_computation.3 | async-start | bytes 5242880 | tf_op jit(solution)/shard_map/reduce_scatter | solution.py:104
  53.1 49.2 %copy-start.1 = (bf16[128,16,256]{2,1,0:T(8,128)(2,1)}, bf16[128,16,256]{2,1,0:T(8,128)(2,1)S(1)}, u32[]{:S(2)}) copy-start(bf16[128,16,256]{2,1,0:T(8,128)(2,1)S(1)} %broadcast_select_fusion.1) | copy-start | bytes 3145732
  53.1 14.3 %collective-permute-start = (bf16[2048,256]{1,0:T(8,128)(2,1)S(1)}, bf16[2048,256]{1,0:T(8,128)(2,1)S(1)}, u32[]{:S(2)}, u32[]{:S(2)}) collective-permute-start(bf16[2048,256]{1,0:T(8,128)(2,1)S(1)} %bitcast.43), channel_id=1, source_target_pairs={{0,1},{1,2},{2,3},{3,0},{4,5},{5,6},{6,7},{7,4},{8,9},{9,10},{10,1... | collective-permute-start | bytes 3145736 | tf_op jit(solution)/shard_map/ppermute | solution.py:78
  67.4 14.3 %collective-permute-start.1 = (bf16[2048,256]{1,0:T(8,128)(2,1)S(1)}, bf16[2048,256]{1,0:T(8,128)(2,1)}, u32[]{:S(2)}, u32[]{:S(2)}) collective-permute-start(bf16[2048,256]{1,0:T(8,128)(2,1)S(1)} %collective-permute-done), channel_id=1, source_target_pairs={{0,1},{1,2},{2,3},{3,0},{4,5},{5,6},{6,7},{7,4},{8,9},{9,10},{10,1... | collective-permute-start | bytes 3145736 | tf_op jit(solution)/shard_map/ppermute | solution.py:78
  81.7 14.5 %collective-permute-start.2 = (bf16[2048,256]{1,0:T(8,128)(2,1)}, bf16[2048,256]{1,0:T(8,128)(2,1)}, u32[]{:S(2)}, u32[]{:S(2)}) collective-permute-start(bf16[2048,256]{1,0:T(8,128)(2,1)} %collective-permute-done.1), channel_id=1, source_target_pairs={{0,1},{1,2},{2,3},{3,0},{4,5},{5,6},{6,7},{7,4},{8,9},{9,10},{10,1... | collective-permute-start | bytes 3145736 | tf_op jit(solution)/shard_map/ppermute | solution.py:78
  102.4 3.2 %copy-start.5 = (bf16[1024,256]{1,0:T(8,128)(2,1)S(1)}, bf16[1024,256]{1,0:T(8,128)(2,1)}, u32[]{:S(2)}) copy-start(bf16[1024,256]{1,0:T(8,128)(2,1)} %param.16) | copy-start | bytes 1572868
  104.4 3.5 %copy-start.6 = (bf16[1024,256]{1,0:T(8,128)(2,1)S(1)}, bf16[1024,256]{1,0:T(8,128)(2,1)}, u32[]{:S(2)}) copy-start(bf16[1024,256]{1,0:T(8,128)(2,1)} %param.17) | copy-start | bytes 1572868
  107.9 2.3 copy-start.7
  110.3 2.3 copy-start.3
  211.2 47.7 %copy-start.2 = (bf16[128,16,256]{2,1,0:T(8,128)(2,1)S(1)}, bf16[128,16,256]{2,1,0:T(8,128)(2,1)}, u32[]{:S(2)}) copy-start(bf16[128,16,256]{2,1,0:T(8,128)(2,1)} %copy-done.1) | copy-start | bytes 3145732
Sparse Core Ops, SparseCore 0:
  215.7 43.2 reduce-scatter.1
